TPU v7x, 256 devices: a whole 4x4x8 slice. The times are simulated.
256 devices in a mesh: tile: 16 (over y, z_hi), head: 16 (over x, z_lo, core).
Axes of the slice: x: 4, y: 4, z: 8 (z_hi: 4, z_lo: 2; z = z_hi * 2 + z_lo), core: 2. Of those that a mesh axis runs over, the one named last changes fastest.
Arguments:
- tokens: bfloat16 [6144, 3072], P('tile'), may hold values from -200 to 200
- mod_shift: float32 [3072], replicated, may hold values from -3 to 3
- mod_scale: float32 [3072], replicated, may hold values from -2.5 to 2.5
- mod_gate: float32 [3072], replicated, may hold values from -4 to 4
- qkv_weight: bfloat16 [3072, 6144], P(None, 'head'), may hold values from -1 to 1
- out_weight: bfloat16 [2048, 3072], P('head'), may hold values from -0.125 to 0.125
- teacher: bfloat16 [6144, 3072], P('tile'), may hold values from -6 to 6
- slot_tiles: int32 [16], replicated, may hold values from 0 to 15, each once
Outputs:
- qkv_grad: float32 [3072, 6144], P('tile', 'head')
- out_grad: float32 [2048, 3072], P('head', 'tile')
Inputs may be any that keep to these rules, and one draw needn't show every extreme that they name: Slot s, rows s * 384 to (s + 1) * 384 - 1 of tokens and teacher, holds tile slot_tiles[s]; every tile once.
All inputs are finite; a program needn't handle non-finite values.
Results may differ from a plain program's by a relative error of at most 0.00049.
Values may be sent and summed in bfloat16 or wider, within the bound.
A program may use at most 128 MiB of HBM per device.

v0:
```python
import math
import jax
import jax.numpy as jnp
from jax import lax
from jax.sharding import PartitionSpec as P

HD = 128
TOK_TILE = 384
TT = 1
TH = 4
EPS_NORM = 1e-05
EPS_ROOT = 1e-06
LOSS_WEIGHT = 32.0


def modulated_norm(tokens, mod_shift, mod_scale):
    values_in = tokens.astype(jnp.float32)
    center = values_in - jnp.mean(values_in, -1, keepdims=True)
    spread = jnp.mean(center * center, -1, keepdims=True)
    return (center * lax.rsqrt(spread + EPS_NORM) * (1.0 + mod_scale) + mod_shift).astype(
        jnp.bfloat16
    )


def root_norm(values):
    factor = lax.rsqrt(jnp.mean(values * values, -1, keepdims=True) + EPS_ROOT)
    return (values * factor, factor)


def root_norm_back(grad_unit, unit_value, factor):
    return factor * (grad_unit - unit_value * jnp.mean(grad_unit * unit_value, -1, keepdims=True))


def tiles_of(slot_tiles, slot_ids):
    onehot = (
        slot_ids[:, None] == jnp.arange(slot_tiles.shape[0], dtype=jnp.int32)[None, :]
    ).astype(jnp.int32)
    return jnp.sum(onehot * slot_tiles[None, :], 1)


def near_tiles(first_tiles, second_tiles, width_tiles):

    def coords(ids):
        return (ids // (TH * width_tiles), ids // width_tiles % TH, ids % width_tiles)

    ta, ha, wa = coords(first_tiles[:, None])
    tb, hb, wb = coords(second_tiles[None, :])
    close = (jnp.abs(ta - tb) <= 1) & (jnp.abs(ha - hb) <= 1) & (jnp.abs(wa - wb) <= 1)
    return close.astype(jnp.float32)


def masked_exp(queries, keys, tile_mask, group_rows):
    att_scale = 1.0 / math.sqrt(HD)
    scores = (
        jnp.einsum("qhd,khd->hqk", queries, keys, preferred_element_type=jnp.float32) * att_scale
    )
    head_count, query_count, key_count = scores.shape
    shaped = jnp.exp(scores).reshape(
        head_count, query_count // group_rows, group_rows, key_count // TOK_TILE, TOK_TILE
    )
    shaped = shaped * tile_mask[None, :, None, :, None]
    return shaped.reshape(head_count, query_count, key_count)


def per_device(tokens, mod_shift, mod_scale, mod_gate, qkv_weight, out_weight, teacher, slot_tiles):
    tok_rows = tokens.shape[0]
    local_tiles = tok_rows // TOK_TILE
    head_count = out_weight.shape[0] // HD
    width_tiles = slot_tiles.shape[0] // (TT * TH)
    att_scale = 1.0 / math.sqrt(HD)
    normed = modulated_norm(tokens, mod_shift, mod_scale)
    projected = jnp.dot(normed, qkv_weight, preferred_element_type=jnp.float32).reshape(
        tok_rows, head_count, 3, HD
    )
    query_unit, query_factor = root_norm(projected[:, :, 0])
    key_unit, key_factor = root_norm(projected[:, :, 1])
    query_b = query_unit.astype(jnp.bfloat16)
    key_b = key_unit.astype(jnp.bfloat16)
    value_b = projected[:, :, 2].astype(jnp.bfloat16)
    all_keys, all_values = (
        lax.all_gather(key_b, "tile", axis=0, tiled=True),
        lax.all_gather(value_b, "tile", axis=0, tiled=True),
    )
    my_slots = lax.axis_index("tile") * local_tiles + jnp.arange(local_tiles, dtype=jnp.int32)
    my_tiles = tiles_of(slot_tiles, my_slots)
    tile_mask = near_tiles(my_tiles, slot_tiles, width_tiles)
    exp_scores = masked_exp(query_b, all_keys, tile_mask, TOK_TILE)
    totals = jnp.sum(exp_scores, -1)
    att_probs = exp_scores / totals[:, :, None]
    probs_b = att_probs.astype(jnp.bfloat16)
    attended = jnp.einsum(
        "hqk,khd->qhd", probs_b, all_values, preferred_element_type=jnp.float32
    ).astype(jnp.bfloat16)
    flat_att = attended.reshape(tok_rows, head_count * HD)
    partial_branch = jnp.dot(flat_att, out_weight, preferred_element_type=jnp.float32)
    whole_branch = lax.psum(partial_branch, "head")
    residual = LOSS_WEIGHT * (mod_gate * whole_branch - teacher.astype(jnp.float32))
    grad_branch = (mod_gate * residual).astype(jnp.bfloat16)
    contract_rows = (((0,), (0,)), ((), ()))
    out_term = lax.dot_general(
        flat_att, grad_branch, contract_rows, preferred_element_type=jnp.float32
    )
    grad_att = lax.dot_general(
        grad_branch, out_weight, (((1,), (1,)), ((), ())), preferred_element_type=jnp.float32
    )
    grad_att = grad_att.reshape(tok_rows, head_count, HD).astype(jnp.bfloat16)
    row_delta = jnp.sum(grad_att.astype(jnp.float32) * attended.astype(jnp.float32), -1)
    grad_probs = jnp.einsum(
        "qhd,khd->hqk", grad_att, all_values, preferred_element_type=jnp.float32
    )
    grad_scores = (att_probs * (grad_probs - row_delta.T[:, :, None])).astype(jnp.bfloat16)
    grad_query_unit = (
        jnp.einsum("hqk,khd->qhd", grad_scores, all_keys, preferred_element_type=jnp.float32)
        * att_scale
    )
    key_terms = (
        jnp.einsum("hqk,qhd->khd", grad_scores, query_b, preferred_element_type=jnp.float32)
        * att_scale
    )
    value_terms = jnp.einsum("hqk,qhd->khd", probs_b, grad_att, preferred_element_type=jnp.float32)
    grad_key_unit, grad_value = (
        lax.psum_scatter(key_terms, "tile", scatter_dimension=0, tiled=True),
        lax.psum_scatter(value_terms, "tile", scatter_dimension=0, tiled=True),
    )
    grad_query = root_norm_back(grad_query_unit, query_unit, query_factor)
    grad_key = root_norm_back(grad_key_unit, key_unit, key_factor)
    grad_qkv = (
        jnp.stack([grad_query, grad_key, grad_value], 2)
        .astype(jnp.bfloat16)
        .reshape(tok_rows, head_count * 3 * HD)
    )
    qkv_term = lax.dot_general(normed, grad_qkv, contract_rows, preferred_element_type=jnp.float32)
    qkv_grad, out_grad = (
        lax.psum_scatter(qkv_term, "tile", scatter_dimension=0, tiled=True),
        lax.psum_scatter(out_term, "tile", scatter_dimension=1, tiled=True),
    )
    return (qkv_grad, out_grad)


def solution(mesh):
    return jax.shard_map(
        per_device,
        mesh=mesh,
        in_specs=(
            P("tile", None),
            P(),
            P(),
            P(),
            P(None, "head"),
            P("head", None),
            P("tile", None),
            P(),
        ),
        out_specs=(P("tile", "head"), P("head", "tile")),
        check_vma=False,
    )
```

profile of v0, /device:TPU:1, one launch (start us, length us, event | category | flops | bytes accessed | tf_op | source)
XLA Modules:
  0.0 681.5 jit_solution(16059884396941234523)
XLA Ops:
  7.3 2.2 convert_reduce_fusion
  9.5 2.4 fusion.3
  12.0 1.7 fusion.47
  15.2 0.7 fusion.39
  18.8 57.1 %all-gather.4.cloned.1.call-done = bf16[6144,1,128]{0,2,1:T(8,128)(2,1)} async-done(((bf16[384,1,128]{0,2,1:T(8,128)(2,1)}), bf16[6144,1,128]{0,2,1:T(8,128)(2,1)}) %all-gather.4.cloned.1.call-update) | async-done | bytes 1572880 | tf_op jit(solution)/shard_map/all_gather | solution.py:81
  76.0 7.2 %fusion.49 = (f32[384]{0:T(512)S(1)}, f32[384,6144]{1,0:T(8,128)}) fusion(f32[6144]{0:T(1024)S(1)} %mul.243, bf16[6144,1,128]{0,2,1:T(8,128)(2,1)} %all-gather.4.cloned.1.call-done, f32[384,1,3,128]{0,3,2,1:T(8,128)S(1)} %bitcast.101, f32[384]{0:T(512)S(1)} %add_rsqrt_fusion.1), kind=kOutput, calls=%fused_computation.80 | convolution fusion | flops 611155584 | bytes 11234816 | tf_op jit(solution)/shard_map/qhd,khd->hqk/dot_general | solution.py:55
  83.2 52.0 %all-gather.6.cloned.1.call-done = bf16[6144,1,1,128]{0,3,2,1:T(8,128)(2,1)} async-done(((bf16[384,1,1,128]{0,3,2,1:T(8,128)(2,1)}), bf16[6144,1,1,128]{0,3,2,1:T(8,128)(2,1)}) %all-gather.6.cloned.1.call-update) | async-done | bytes 1572880 | tf_op jit(solution)/shard_map/all_gather | solution.py:82
  135.2 5.8 fusion.21
  141.0 2.9 fusion.35
  144.1 139.6 %all-reduce.2.cloned.1.call-done = f32[384,3072]{1,0:T(8,128)} async-done(((f32[384,3072]{1,0:T(8,128)}), f32[384,3072]{1,0:T(8,128)}) %all-reduce.2.cloned.1.call-update) | async-done | bytes 4718608 | tf_op jit(solution)/shard_map/psum | solution.py:96
  283.6 4.0 multiply_convert_fusion.1
  287.6 0.8 fusion.26
  289.0 4.6 multiply_convert_fusion
  293.7 2.2 copy-done.1
  295.9 2.6 fusion
  298.6 6.4 convolution_bitcast_fusion
  305.3 3.9 fusion.33
  309.2 81.2 %reduce-scatter.5.cloned.1.call-done = f32[384,1,128]{0,2,1:T(8,128)} async-done(((f32[6144,1,128]{0,2,1:T(8,128)}), f32[384,1,128]{0,2,1:T(8,128)}) %reduce-scatter.5.cloned.1.call-update) | async-done | bytes 196624 | tf_op jit(solution)/shard_map/reduce_scatter | solution.py:122
  390.4 4.4 multiply_reduce_fusion.1
  394.8 88.3 %reduce-scatter.7.cloned.1.call-done = f32[384,1,128]{0,2,1:T(8,128)} async-done(((f32[6144,1,128]{0,2,1:T(8,128)}), f32[384,1,128]{0,2,1:T(8,128)}) %reduce-scatter.7.cloned.1.call-update) | async-done | bytes 196624 | tf_op jit(solution)/shard_map/reduce_scatter | solution.py:123
  483.1 0.9 convert_bitcast_fusion
  484.2 5.6 fusion.45
  489.8 81.3 %reduce-scatter.11.cloned.1.call-done = f32[128,192]{0,1:T(8,128)} async-done(((f32[128,3072]{0,1:T(8,128)}), f32[128,192]{0,1:T(8,128)}) %reduce-scatter.11.cloned.1.call-update) | async-done | bytes 98320 | tf_op jit(solution)/shard_map/reduce_scatter | solution.py:135
  571.1 103.6 %reduce-scatter.9.cloned.1.call-done = f32[192,384]{1,0:T(8,128)} async-done(((f32[3072,384]{1,0:T(8,128)}), f32[192,384]{1,0:T(8,128)}) %reduce-scatter.9.cloned.1.call-update) | async-done | bytes 294928 | tf_op jit(solution)/shard_map/reduce_scatter | solution.py:134
  (52 shorter events, 2.8 us)
Async XLA Ops:
  7.2 4.8 copy-start
  7.2 4.7 copy-start.8
  7.2 4.7 copy-start.11
  7.2 68.8 %all-gather.4.cloned.1.call-start = ((), (), s32[]{:S(2)}) async-start(), calls=%async_computation.4 | async-start | bytes 1671168 | tf_op jit(solution)/shard_map/all_gather | solution.py:81
  7.2 4.7 copy-start.2
  12.0 3.2 copy-start.9
  14.4 120.8 %all-gather.6.cloned.1.call-start = ((), (), s32[]{:S(2)}) async-start(), calls=%async_computation.10 | async-start | bytes 1671168 | tf_op jit(solution)/shard_map/all_gather | solution.py:82
  15.1 268.5 %all-reduce.2.cloned.1.call-start = ((), (), s32[]{:S(2)}) async-start(), calls=%async_computation.5 | async-start | bytes 9437184 | tf_op jit(solution)/shard_map/psum | solution.py:96
  135.2 5.8 copy-start.4
  141.0 3.0 copy-start.7
  144.0 246.4 %reduce-scatter.5.cloned.1.call-start = ((), (), s32[]{:S(2)}) async-start(), calls=%async_computation.6 | async-start | bytes 3342336 | tf_op jit(solution)/shard_map/reduce_scatter | solution.py:122
  283.6 4.0 copy-start.5
  283.6 5.4 copy-start.10
  287.6 1.4 copy-start.3
  293.7 2.2 copy-start.1
  298.6 184.5 %reduce-scatter.7.cloned.1.call-start = ((), (), s32[]{:S(2)}) async-start(), calls=%async_computation.7 | async-start | bytes 3342336 | tf_op jit(solution)/shard_map/reduce_scatter | solution.py:123
  305.0 266.1 %reduce-scatter.11.cloned.1.call-start = ((), (), s32[]{:S(2)}) async-start(), calls=%async_computation.9 | async-start | bytes 1671168 | tf_op jit(solution)/shard_map/reduce_scatter | solution.py:135
  309.2 365.5 %reduce-scatter.9.cloned.1.call-start = ((), (), s32[]{:S(2)}) async-start(), calls=%async_computation.8 | async-start | bytes 5013504 | tf_op jit(solution)/shard_map/reduce_scatter | solution.py:134
  390.4 93.7 %copy-start.6 = (f32[384,1,128]{0,2,1:T(8,128)S(1)}, f32[384,1,128]{0,2,1:T(8,128)}, u32[]{:S(2)}) copy-start(f32[384,1,128]{0,2,1:T(8,128)} %reduce-scatter.5.cloned.1.call-done) | copy-start | bytes 589828
Sparse Core Ops, SparseCore 0:
  14.5 61.4 all-gather.3
  78.9 56.1 all-gather.5
  144.1 139.4 all-reduce.1
  298.7 91.6 reduce-scatter.4
  393.9 89.1 reduce-scatter.6
  487.1 83.9 reduce-scatter.10
  575.3 99.3 reduce-scatter.8
where the time goes:
time: 682 us
  waiting for transfers between devices  603 us (88%)
  matrix products  46 us (7%)
  between operations  17.2 us (3%)
  other arithmetic  11.1 us (2%)
    psum x1, waiting for transfers between devices, per_device(): whole_branch = lax.psum(partial_branch, 'head')  140 us
    reduce_scatter x1, waiting for transfers between devices, per_device(): lax.psum_scatter(qkv_term, 'tile', scatter_dimension=0, tiled=True)  104 us
    reduce_scatter x1, waiting for transfers between devices, per_device(): lax.psum_scatter(value_terms, 'tile', scatter_dimension=0, tiled=True)  88.3 us
    reduce_scatter x1, waiting for transfers between devices, per_device(): lax.psum_scatter(out_term, 'tile', scatter_dimension=1, tiled=True)  81.3 us
    reduce_scatter x1, waiting for transfers between devices, per_device(): lax.psum_scatter(key_terms, 'tile', scatter_dimension=0, tiled=True)  81.2 us
    all_gather x1, waiting for transfers between devices, per_device(): lax.all_gather(key_b, 'tile', axis=0, tiled=True)  57.1 us
    all_gather x1, waiting for transfers between devices, per_device(): lax.all_gather(value_b, 'tile', axis=0, tiled=True)  52 us
  transfers between devices with their start and end apart: 7, of which 7 were waited for; matrix products, arithmetic and copies ran while one was open for 4% of the time, Pallas kernels for 0%

commit v1 on v0

--- a/solution.py
+++ b/solution.py
@@ -93,7 +93,7 @@
     ).astype(jnp.bfloat16)
     flat_att = attended.reshape(tok_rows, head_count * HD)
     partial_branch = jnp.dot(flat_att, out_weight, preferred_element_type=jnp.float32)
-    whole_branch = lax.psum(partial_branch, "head")
+    whole_branch = jnp.sum(lax.all_gather(partial_branch, "head"), axis=0)
     residual = LOSS_WEIGHT * (mod_gate * whole_branch - teacher.astype(jnp.float32))
     grad_branch = (mod_gate * residual).astype(jnp.bfloat16)
     contract_rows = (((0,), (0,)), ((), ()))

time: 682 us -> 937 us (1.37)
  waiting for transfers between devices: 603 us -> 833 us
  other arithmetic: 11.1 us -> 36.9 us
    all_gather x0 -> x1, waiting for transfers between devices: none -> 370 us  [per_device(): whole_branch = jnp.sum(lax.all_gather(partial_branch, 'head'), axis=0)]
    psum x1 -> x0, waiting for transfers between devices: 140 us -> none  [per_device(): whole_branch = lax.psum(partial_branch, 'head')]
    reduce_sum x0 -> x1, other arithmetic: none -> 25.7 us  [per_device(): whole_branch = jnp.sum(lax.all_gather(partial_branch, 'head'), axis=0)]
  transfers between devices with their start and end apart: 7 -> 7, of which waited for: 7 -> 7; matrix products, arithmetic and copies ran while one was open for 4% -> 3% of each run, Pallas kernels for 0% -> 0%
where the time goes in v1:
time: 937 us
  waiting for transfers between devices  833 us (89%)
  matrix products  46.3 us (5%)
  other arithmetic  36.9 us (4%)
  between operations  17.2 us (2%)
    all_gather x1, waiting for transfers between devices, per_device(): whole_branch = jnp.sum(lax.all_gather(partial_branch, 'head'), axis=0)  370 us
    reduce_scatter x1, waiting for transfers between devices, per_device(): lax.psum_scatter(qkv_term, 'tile', scatter_dimension=0, tiled=True)  104 us
    reduce_scatter x1, waiting for transfers between devices, per_device(): lax.psum_scatter(value_terms, 'tile', scatter_dimension=0, tiled=True)  88.4 us
    reduce_scatter x1, waiting for transfers between devices, per_device(): lax.psum_scatter(out_term, 'tile', scatter_dimension=1, tiled=True)  81.1 us
    reduce_scatter x1, waiting for transfers between devices, per_device(): lax.psum_scatter(key_terms, 'tile', scatter_dimension=0, tiled=True)  79.9 us
    all_gather x1, waiting for transfers between devices, per_device(): lax.all_gather(key_b, 'tile', axis=0, tiled=True)  57.1 us
    all_gather x1, waiting for transfers between devices, per_device(): lax.all_gather(value_b, 'tile', axis=0, tiled=True)  51.9 us
    reduce_sum x1, other arithmetic, per_device(): whole_branch = jnp.sum(lax.all_gather(partial_branch, 'head'), axis=0)  25.7 us
  transfers between devices with their start and end apart: 7, of which 7 were waited for; matrix products, arithmetic and copies ran while one was open for 3% of the time, Pallas kernels for 0%

profile of v1, /device:TPU:1, one launch (start us, length us, event | category | flops | bytes accessed | tf_op | source)
XLA Modules:
  0.0 937.0 jit_solution(5755387117305677894)
XLA Ops:
  7.3 2.2 convert_reduce_fusion
  9.5 2.4 fusion.3
  12.0 1.7 fusion.47
  18.8 57.1 %all-gather.6.cloned.1.call-done = bf16[6144,1,128]{0,2,1:T(8,128)(2,1)} async-done(((bf16[384,1,128]{0,2,1:T(8,128)(2,1)}), bf16[6144,1,128]{0,2,1:T(8,128)(2,1)}) %all-gather.6.cloned.1.call-update) | async-done | bytes 1572880 | tf_op jit(solution)/shard_map/all_gather | solution.py:81
  76.0 7.3 fusion.49
  83.3 51.9 %all-gather.8.cloned.1.call-done = bf16[6144,1,1,128]{0,3,2,1:T(8,128)(2,1)} async-done(((bf16[384,1,1,128]{0,3,2,1:T(8,128)(2,1)}), bf16[6144,1,1,128]{0,3,2,1:T(8,128)(2,1)}) %all-gather.8.cloned.1.call-update) | async-done | bytes 1572880 | tf_op jit(solution)/shard_map/all_gather | solution.py:82
  135.2 5.8 fusion.21
  141.0 3.0 fusion.35
  144.1 369.8 %all-gather.10.cloned.1.call-done = f32[6144,3072]{1,0:T(8,128)} async-done(((f32[384,3072]{1,0:T(8,128)}), f32[6144,3072]{1,0:T(8,128)}) %all-gather.10.cloned.1.call-update) | async-done | bytes 75497488 | tf_op jit(solution)/shard_map/all_gather | solution.py:96
  514.0 25.7 %reduce_sum.96 = f32[384,3072]{1,0:T(8,128)} reduce(f32[16,384,3072]{2,1,0:T(8,128)} %bitcast.13, f32[]{:T(128)} %constant.101.clone.1), dimensions={0}, to_apply=%region_6.7 | reduce | flops 17694720 | bytes 80216064 | tf_op jit(solution)/shard_map/reduce_sum | solution.py:96
  539.7 4.0 multiply_convert_fusion.1
  543.7 0.8 fusion.26
  545.2 4.6 multiply_convert_fusion
  549.8 2.1 copy-done.1
  552.0 2.7 fusion
  555.0 6.4 convolution_bitcast_fusion
  561.4 3.9 fusion.33
  565.4 79.9 %reduce-scatter.5.cloned.1.call-done = f32[384,1,128]{0,2,1:T(8,128)} async-done(((f32[6144,1,128]{0,2,1:T(8,128)}), f32[384,1,128]{0,2,1:T(8,128)}) %reduce-scatter.5.cloned.1.call-update) | async-done | bytes 196624 | tf_op jit(solution)/shard_map/reduce_scatter | solution.py:122
  645.3 4.4 multiply_reduce_fusion.1
  649.7 88.4 %reduce-scatter.7.cloned.1.call-done = f32[384,1,128]{0,2,1:T(8,128)} async-done(((f32[6144,1,128]{0,2,1:T(8,128)}), f32[384,1,128]{0,2,1:T(8,128)}) %reduce-scatter.7.cloned.1.call-update) | async-done | bytes 196624 | tf_op jit(solution)/shard_map/reduce_scatter | solution.py:123
  738.1 0.9 convert_bitcast_fusion
  739.2 5.6 fusion.45
  744.8 81.1 %reduce-scatter.11.cloned.1.call-done = f32[128,192]{0,1:T(8,128)} async-done(((f32[128,3072]{0,1:T(8,128)}), f32[128,192]{0,1:T(8,128)}) %reduce-scatter.11.cloned.1.call-update) | async-done | bytes 98320 | tf_op jit(solution)/shard_map/reduce_scatter | solution.py:135
  825.9 104.2 %reduce-scatter.9.cloned.1.call-done = f32[192,384]{1,0:T(8,128)} async-done(((f32[3072,384]{1,0:T(8,128)}), f32[192,384]{1,0:T(8,128)}) %reduce-scatter.9.cloned.1.call-update) | async-done | bytes 294928 | tf_op jit(solution)/shard_map/reduce_scatter | solution.py:134
  (53 shorter events, 3.6 us)
Async XLA Ops:
  7.2 4.8 copy-start
  7.2 4.7 copy-start.8
  7.2 4.7 copy-start.11
  7.2 68.8 %all-gather.6.cloned.1.call-start = ((), (), s32[]{:S(2)}) async-start(), calls=%async_computation.4 | async-start | bytes 1671168 | tf_op jit(solution)/shard_map/all_gather | solution.py:81
  7.2 4.7 copy-start.2
  12.0 3.2 copy-start.9
  14.4 120.8 %all-gather.8.cloned.1.call-start = ((), (), s32[]{:S(2)}) async-start(), calls=%async_computation.9 | async-start | bytes 1671168 | tf_op jit(solution)/shard_map/all_gather | solution.py:82
  15.1 498.8 %all-gather.10.cloned.1.call-start = ((), (), s32[]{:S(2)}) async-start(), calls=%async_computation.10 | async-start | bytes 80216064 | tf_op jit(solution)/shard_map/all_gather | solution.py:96
  135.2 5.8 copy-start.4
  141.0 3.1 copy-start.7
  144.1 501.2 %reduce-scatter.5.cloned.1.call-start = ((), (), s32[]{:S(2)}) async-start(), calls=%async_computation.5 | async-start | bytes 3342336 | tf_op jit(solution)/shard_map/reduce_scatter | solution.py:122
  539.7 4.0 copy-start.5
  539.7 5.5 copy-start.10
  543.7 1.5 copy-start.3
  549.8 2.1 copy-start.1
  554.7 183.4 %reduce-scatter.7.cloned.1.call-start = ((), (), s32[]{:S(2)}) async-start(), calls=%async_computation.6 | async-start | bytes 3342336 | tf_op jit(solution)/shard_map/reduce_scatter | solution.py:123
  561.4 264.5 %reduce-scatter.11.cloned.1.call-start = ((), (), s32[]{:S(2)}) async-start(), calls=%async_computation.8 | async-start | bytes 1671168 | tf_op jit(solution)/shard_map/reduce_scatter | solution.py:135
  565.3 364.8 %reduce-scatter.9.cloned.1.call-start = ((), (), s32[]{:S(2)}) async-start(), calls=%async_computation.7 | async-start | bytes 5013504 | tf_op jit(solution)/shard_map/reduce_scatter | solution.py:134
  645.3 93.8 %copy-start.6 = (f32[384,1,128]{0,2,1:T(8,128)S(1)}, f32[384,1,128]{0,2,1:T(8,128)}, u32[]{:S(2)}) copy-start(f32[384,1,128]{0,2,1:T(8,128)} %reduce-scatter.5.cloned.1.call-done) | copy-start | bytes 589828
Sparse Core Ops, SparseCore 0:
  14.5 61.4 all-gather.5
  78.9 56.1 all-gather.7
  144.2 369.7 all-gather.9
  554.8 90.4 reduce-scatter.4
  648.8 89.3 reduce-scatter.6
  742.1 83.8 reduce-scatter.10
  830.1 99.9 reduce-scatter.8
